TPU v7x, 256 devices: a whole 4x4x8 slice. The times are simulated.
256 devices in a mesh: grp: 64 (over z, y, core), head: 4 (over x).
Axes of the slice: x: 4, y: 4, z: 8, core: 2. Of those that a mesh axis runs over, the one named last changes fastest.
Arguments:
- arriving_hiddens: bfloat16 [512, 4, 2048], P('grp', None, 'head'), may hold values from -6 to 6
- occupied_slot_totals: int32 [512], P('grp'), may hold values from 1 to 4
- former_indices: int32 [512], P('grp'), may hold values from 0 to 511, as said below
- reconstruct_marks: int32 [512], P('grp'), may hold values from 0 to 1, as said below
- retained_hiddens: bfloat16 [512, 32, 2048], P('grp', None, 'head'), may hold values from -6 to 6
- carried_memory_matrices: float32 [512, 16, 64, 64], P('grp', 'head'), may hold values from -12 to 12
- lagged_previous_entries: float32 [512, 2, 2048], P('grp', None, 'head'), may hold values from -6 to 6
- pre_attention_scaling: float32 [2048], replicated, may hold values from 0.5 to 1.5
- pre_feedforward_scaling: float32 [2048], replicated, may hold values from 0.5 to 1.5
- lag_blend_fractions: float32 [5, 2048], replicated, may hold values from 0 to 1
- acceptance_projection: bfloat16 [2048, 1024], P(None, 'head'), may hold values from -0.125 to 0.125
- address_projection: bfloat16 [2048, 1024], P(None, 'head'), may hold values from -0.125 to 0.125
- content_projection: bfloat16 [2048, 1024], P(None, 'head'), may hold values from -0.125 to 0.125
- fading_lowrank_left: bfloat16 [2048, 64], replicated, may hold values from -0.125 to 0.125
- fading_lowrank_right: bfloat16 [64, 1024], P(None, 'head'), may hold values from -0.75 to 0.75
- fading_baseline_entries: float32 [1024], P('head'), may hold values from -6 to 1
- present_item_reward: float32 [1024], P('head'), may hold values from -6 to 6
- grouped_layer_scaling: float32 [1024], P('head'), may hold values from 0.5 to 1.5
- attention_exit_projection: bfloat16 [1024, 2048], P('head'), may hold values from -0.1875 to 0.1875
- feedforward_address_proj: bfloat16 [2048, 3584], P(None, 'head'), may hold values from -0.125 to 0.125
- feedforward_content_proj: bfloat16 [3584, 2048], P('head'), may hold values from -0.09375 to 0.09375
Outputs:
- next_tokens: bfloat16 [512, 4, 2048], P('grp', None, 'head')
- next_state: float32 [512, 16, 64, 64], P('grp', 'head')
- next_shift: float32 [512, 2, 2048], P('grp', None, 'head')
Inputs may be any that keep to these rules, and one draw needn't show every extreme that they name: former_indices[g * 8 + j] = ((g + offset_j) mod 64) * 8 + local_j, where the 8 offsets offset_j are distinct numbers of 0 to 63 and local_j is a permutation of 0 to 7, both the same for every group g. `reconstruct_marks`: among the 8 requests of one group at most 2 are marked, and some group has exactly 2.
All inputs are finite; a program needn't handle non-finite values.
Results may differ from a plain program's by a relative error of at most 0.028.
Values may be sent and summed in bfloat16 or wider, within the bound.
No kernel may reach another device: no remote copies, remote signals or barrier semaphores. Data moves between devices by JAX's collectives and lax.ppermute only.
A program may use at most 128 MiB of HBM per device.

v0:
```python
import jax
import jax.numpy as jnp
from jax import lax
from jax.sharding import PartitionSpec as P

ATTENTION_WIDTH = 64
REB = 2
EPSILON = 1e-05


def shifted_2(value, axis, steps):
    count = lax.axis_size(axis)
    pairs = [(source, (source + steps) % count) for source in range(count)]
    return lax.ppermute(value, axis, pairs)


def layer_norm(inputs, gain):
    centered = inputs - jnp.mean(inputs, axis=-1, keepdims=True)
    spread = jnp.mean(centered * centered, axis=-1, keepdims=True)
    return (centered * lax.rsqrt(spread + EPSILON) * gain).astype(jnp.bfloat16)


def blend_rows(current, previous, rate):
    return (current + (previous - current) * rate).astype(jnp.bfloat16)


def project(inputs, weight):
    flat_rows = inputs.reshape(-1, inputs.shape[-1])
    result = jnp.dot(flat_rows, weight, preferred_element_type=jnp.float32)
    return result.reshape(inputs.shape[:-1] + (weight.shape[1],))


def divide_into_groups(inputs):
    return inputs.reshape(inputs.shape[:-1] + (-1, ATTENTION_WIDTH))


def key_value_decay(
    current,
    previous,
    lag_blend_fractions,
    address_projection,
    content_projection,
    fading_lowrank_left,
    fading_lowrank_right,
    fading_baseline_entries,
):
    key_rows = project(blend_rows(current, previous, lag_blend_fractions[1]), address_projection)
    values = project(blend_rows(current, previous, lag_blend_fractions[2]), content_projection)
    lowrank = jnp.tanh(
        project(blend_rows(current, previous, lag_blend_fractions[3]), fading_lowrank_left)
    ).astype(jnp.bfloat16)
    decay_rates = jnp.exp(
        -jnp.exp(fading_baseline_entries + project(lowrank, fading_lowrank_right))
    )
    return (
        divide_into_groups(key_rows),
        divide_into_groups(values),
        divide_into_groups(decay_rates),
    )


def advance(present_outer_product, inputs):
    key_step, value_step, decay_step = inputs
    return (
        decay_step[..., :, None] * present_outer_product
        + key_step[..., :, None] * value_step[..., None, :],
        None,
    )


def rebuild(
    retained_hiddens,
    pre_attention_scaling,
    lag_blend_fractions,
    address_projection,
    content_projection,
    fading_lowrank_left,
    fading_lowrank_right,
    fading_baseline_entries,
):
    standardized_entry = layer_norm(retained_hiddens.astype(jnp.float32), pre_attention_scaling)
    current = standardized_entry.astype(jnp.float32)
    previous = jnp.concatenate([jnp.zeros_like(current[:, :1]), current[:, :-1]], axis=1)
    key_rows, values, decay_rates = key_value_decay(
        current,
        previous,
        lag_blend_fractions,
        address_projection,
        content_projection,
        fading_lowrank_left,
        fading_lowrank_right,
        fading_baseline_entries,
    )
    start_state = jnp.zeros(
        key_rows.shape[:1] + key_rows.shape[2:] + (ATTENTION_WIDTH,), jnp.float32
    )
    final_state, _ = lax.scan(
        advance,
        start_state,
        (jnp.moveaxis(key_rows, 1, 0), jnp.moveaxis(values, 1, 0), jnp.moveaxis(decay_rates, 1, 0)),
    )
    return (final_state, current[:, -1])


def attention_result(
    standardized_entry,
    lagged_entry,
    present_outer_product,
    occupied_slot_totals,
    lag_blend_fractions,
    acceptance_projection,
    address_projection,
    content_projection,
    fading_lowrank_left,
    fading_lowrank_right,
    fading_baseline_entries,
    present_item_reward,
    grouped_layer_scaling,
):
    current = standardized_entry.astype(jnp.float32)
    previous = jnp.concatenate([lagged_entry[:, None], current[:, :-1]], axis=1)
    acceptance_gate_entries = divide_into_groups(
        project(blend_rows(current, previous, lag_blend_fractions[0]), acceptance_projection)
    )
    key_rows, values, decay_rates = key_value_decay(
        current,
        previous,
        lag_blend_fractions,
        address_projection,
        content_projection,
        fading_lowrank_left,
        fading_lowrank_right,
        fading_baseline_entries,
    )
    reward_grouped = divide_into_groups(present_item_reward)
    decoding_results = []
    for query_slot_index in range(current.shape[1]):
        address_content_product = (
            key_rows[:, query_slot_index, :, :, None] * values[:, query_slot_index, :, None, :]
        )
        decoding_results.append(
            jnp.einsum(
                "ghl,ghlm->ghm",
                acceptance_gate_entries[:, query_slot_index],
                present_outer_product + reward_grouped[:, :, None] * address_content_product,
                precision=lax.Precision.HIGHEST,
            )
        )
        valid_rows = (query_slot_index < occupied_slot_totals)[:, None, None, None]
        present_outer_product = jnp.where(
            valid_rows,
            decay_rates[:, query_slot_index, :, :, None] * present_outer_product
            + address_content_product,
            present_outer_product,
        )
    mixed_heads = jnp.stack(decoding_results, axis=1)
    centered = mixed_heads - jnp.mean(mixed_heads, axis=-1, keepdims=True)
    spread = jnp.mean(centered * centered, axis=-1, keepdims=True)
    grouped_results = (
        centered * lax.rsqrt(spread + EPSILON) * divide_into_groups(grouped_layer_scaling)
    ).astype(jnp.bfloat16)
    return (grouped_results.reshape(grouped_results.shape[:2] + (-1,)), present_outer_product)


def last_live(inputs, occupied_slot_totals):
    pick_table = (
        jnp.arange(inputs.shape[1])[None, :, None] == (occupied_slot_totals - 1)[:, None, None]
    )
    return jnp.sum(jnp.where(pick_table, inputs, jnp.zeros_like(inputs)), axis=1)


def on_device(
    arriving_hiddens,
    occupied_slot_totals,
    former_indices,
    reconstruct_marks,
    retained_hiddens,
    carried_memory_matrices,
    lagged_previous_entries,
    pre_attention_scaling,
    pre_feedforward_scaling,
    lag_blend_fractions,
    acceptance_projection,
    address_projection,
    content_projection,
    fading_lowrank_left,
    fading_lowrank_right,
    fading_baseline_entries,
    present_item_reward,
    grouped_layer_scaling,
    attention_exit_projection,
    feedforward_address_proj,
    feedforward_content_proj,
):
    req_rows = arriving_hiddens.shape[0]
    local_heads = carried_memory_matrices.shape[1]
    model_width = pre_attention_scaling.shape[0]
    grp_index = lax.axis_index("grp")
    groups = lax.axis_size("grp")
    head_index = lax.axis_index("head")
    feature_part = model_width // lax.axis_size("head")
    offset = (former_indices // req_rows - grp_index) % groups
    source_row = former_indices % req_rows
    state_size = local_heads * ATTENTION_WIDTH * ATTENTION_WIDTH
    packed = jnp.concatenate(
        [
            carried_memory_matrices.reshape(req_rows, -1),
            lagged_previous_entries.reshape(req_rows, -1),
        ],
        axis=1,
    )
    ready_rows = jnp.take(packed, source_row, axis=0)
    moved_rows = ready_rows
    for bit_index in range((groups - 1).bit_length()):
        shifted = shifted_2(moved_rows, "grp", -(1 << bit_index))
        moved_rows = jnp.where((offset >> bit_index & 1 == 1)[:, None], shifted, moved_rows)
    present_outer_product = moved_rows[:, :state_size].reshape(
        req_rows, local_heads, ATTENTION_WIDTH, ATTENTION_WIDTH
    )
    shift_part = moved_rows[:, state_size:].reshape(req_rows, 2, feature_part)
    mark_rank = jnp.cumsum(reconstruct_marks) - reconstruct_marks
    slot_table = (
        (reconstruct_marks[None, :] == 1) & (mark_rank[None, :] == jnp.arange(REB)[:, None])
    ).astype(jnp.bfloat16)
    chosen = jnp.einsum(
        "sn,ntd->std", slot_table, retained_hiddens, preferred_element_type=jnp.float32
    ).astype(jnp.bfloat16)
    full_tokens, full_chosen = (
        lax.all_gather(arriving_hiddens, "head", axis=2, tiled=True),
        lax.all_gather(chosen, "head", axis=2, tiled=True),
    )
    full_shift = lax.all_gather(shift_part.astype(jnp.bfloat16), "head", axis=2, tiled=True).astype(
        shift_part.dtype
    )
    rebuilt, last_hist = rebuild(
        full_chosen,
        pre_attention_scaling,
        lag_blend_fractions,
        address_projection,
        content_projection,
        fading_lowrank_left,
        fading_lowrank_right,
        fading_baseline_entries,
    )
    pick_slot = jnp.clip(mark_rank, 0, REB - 1)
    marked = reconstruct_marks == 1
    present_outer_product = jnp.where(
        marked[:, None, None, None], jnp.take(rebuilt, pick_slot, axis=0), present_outer_product
    )
    lagged_entry = jnp.where(
        marked[:, None], jnp.take(last_hist, pick_slot, axis=0), full_shift[:, 0]
    )
    standardized_entry = layer_norm(full_tokens.astype(jnp.float32), pre_attention_scaling)
    grouped_results, present_outer_product = attention_result(
        standardized_entry,
        lagged_entry,
        present_outer_product,
        occupied_slot_totals,
        lag_blend_fractions,
        acceptance_projection,
        address_projection,
        content_projection,
        fading_lowrank_left,
        fading_lowrank_right,
        fading_baseline_entries,
        present_item_reward,
        grouped_layer_scaling,
    )
    flat_heads = grouped_results.reshape(-1, grouped_results.shape[-1])
    mix_total = lax.psum(
        jnp.dot(flat_heads, attention_exit_projection, preferred_element_type=jnp.float32).astype(
            jnp.bfloat16
        ),
        "head",
    ).astype(jnp.float32)
    middle = (full_tokens.astype(jnp.float32) + mix_total.reshape(full_tokens.shape)).astype(
        jnp.bfloat16
    )
    middle_local = lax.dynamic_slice_in_dim(middle, head_index * feature_part, feature_part, 2)
    second = layer_norm(middle.astype(jnp.float32), pre_feedforward_scaling)
    current = second.astype(jnp.float32)
    previous = jnp.concatenate([full_shift[:, 1][:, None], current[:, :-1]], axis=1)
    hidden = jnp.square(
        jax.nn.relu(
            project(blend_rows(current, previous, lag_blend_fractions[4]), feedforward_address_proj)
        )
    ).astype(jnp.bfloat16)
    flat_hidden = hidden.reshape(-1, hidden.shape[-1])
    ffn_rows = lax.psum_scatter(
        lax.dot_general(
            feedforward_content_proj,
            flat_hidden,
            (((0,), (1,)), ((), ())),
            preferred_element_type=jnp.float32,
        ).astype(jnp.bfloat16),
        "head",
        scatter_dimension=0,
        tiled=True,
    ).astype(jnp.float32)
    result = (middle_local.astype(jnp.float32) + ffn_rows.T.reshape(middle_local.shape)).astype(
        jnp.bfloat16
    )
    valid_rows = jnp.arange(arriving_hiddens.shape[1])[None, :] < occupied_slot_totals[:, None]
    result = jnp.where(valid_rows[..., None], result, jnp.zeros_like(result))
    time_last = lax.dynamic_slice_in_dim(
        last_live(standardized_entry.astype(jnp.float32), occupied_slot_totals),
        head_index * feature_part,
        feature_part,
        1,
    )
    channel_last = lax.dynamic_slice_in_dim(
        last_live(current, occupied_slot_totals), head_index * feature_part, feature_part, 1
    )
    return (result, present_outer_product, jnp.stack([time_last, channel_last], axis=1))


def solution(mesh):
    placed = (
        P("grp", None, "head"),
        P("grp"),
        P("grp"),
        P("grp"),
        P("grp", None, "head"),
        P("grp", "head", None, None),
        P("grp", None, "head"),
        P(),
        P(),
        P(),
        P(None, "head"),
        P(None, "head"),
        P(None, "head"),
        P(),
        P(None, "head"),
        P("head"),
        P("head"),
        P("head"),
        P("head", None),
        P(None, "head"),
        P("head", None),
    )
    return jax.shard_map(
        on_device,
        mesh=mesh,
        in_specs=placed,
        out_specs=(P("grp", None, "head"), P("grp", "head", None, None), P("grp", None, "head")),
        check_vma=False,
    )
```

profile of v0, /device:TPU:8, one launch (start us, length us, event | category | flops | bytes accessed | tf_op | source)
XLA Modules:
  0.0 305.9 jit_solution(17810951148594460560)
XLA Ops:
  7.2 1.4 and_compare_fusion.5
  9.4 1.6 reshape.289
  15.0 12.6 %all_gather.10 = bf16[2,32,2048]{2,1,0:T(8,128)(2,1)S(1)} all-gather(bf16[2,32,512]{2,1,0:T(8,128)(2,1)S(1)} %copy.145), channel_id=1, replica_groups=mesh['grp'=64,'head'=4] {'head'}, dimensions={2}, use_global_device_ids=true | all-gather | bytes 327680 | tf_op jit(solution)/shard_map/all_gather | solution.py:230
  29.0 1.2 broadcast_select_fusion.1
  30.2 8.3 %collective-permute-start.1 = (f32[8,17408]{1,0:T(8,128)S(1)}, f32[8,17408]{1,0:T(8,128)}, u32[]{:S(2)}, u32[]{:S(2)}) collective-permute-start(f32[8,17408]{1,0:T(8,128)S(1)} %broadcast_select_fusion.1), channel_id=1, source_target_pairs={{0,248},{4,252},{8,0},{12,4},{16,8},{20,12},{24,16},{28,20},{32,24... | collective-permute-start | bytes 1671176 | tf_op jit(solution)/shard_map/ppermute | solution.py:14
  38.5 1.4 fusion.15
  40.1 2.3 copy.80
  42.4 1.5 copy.81
  43.9 2.4 convolution_bitcast_fusion.1
  46.3 2.4 convolution_bitcast_fusion
  48.7 1.4 broadcast_select_fusion.2
  50.0 5.3 %collective-permute-start.2 = (f32[8,17408]{1,0:T(8,128)S(1)}, f32[8,17408]{1,0:T(8,128)}, u32[]{:S(2)}, u32[]{:S(2)}) collective-permute-start(f32[8,17408]{1,0:T(8,128)S(1)} %broadcast_select_fusion.2), channel_id=1, source_target_pairs={{0,240},{4,244},{8,248},{12,252},{16,0},{20,4},{24,8},{28,12},{32,... | collective-permute-start | bytes 1671176 | tf_op jit(solution)/shard_map/ppermute | solution.py:14
  55.4 34.7 %while.11 = (s32[]{:T(128)}, f32[2,4,64,64]{3,2,1,0:T(8,128)S(1)}, f32[32,2,4,64]{3,2,1,0:T(4,128)S(1)}, f32[32,2,4,64]{3,0,2,1:T(8,128)S(1)}, f32[32,2,4,64]{3,0,2,1:T(8,128)}, /*index=5*/s32[]{:T(128)}, s32[]{:T(128)}) while((s32[]{:T(128)}, f32[2,4,64,64]{3,2,1,0:T(8,128)S(1)}, f32[32,2,4,64]{3,2,1,0:T(4,128)S(1)}, ...), condition=%wide.region_6.7_spmd.clone, body=%wide.region_5.6_spmd.clone.sunk | while | flops 131075 | bytes 280679 | solution.py:97
  91.0 1.4 mul.345
  92.4 2.3 copy.77
  94.7 12.0 %all_gather.9 = bf16[8,4,2048]{2,1,0:T(4,128)(2,1)S(1)} all-gather(bf16[8,4,512]{2,1,0:T(4,128)(2,1)S(1)} %copy-done.16), channel_id=1, replica_groups=mesh['grp'=64,'head'=4] {'head'}, dimensions={2}, use_global_device_ids=true | all-gather | bytes 163840 | tf_op jit(solution)/shard_map/all_gather | solution.py:229
  108.7 18.3 %collective-permute-done.3 = f32[8,17408]{1,0:T(8,128)S(1)} collective-permute-done((f32[8,17408]{1,0:T(8,128)S(1)}, f32[8,17408]{1,0:T(8,128)S(1)}, u32[]{:S(2)}, u32[]{:S(2)}) %collective-permute-start.3) | collective-permute-done | bytes 557088 | tf_op jit(solution)/shard_map/ppermute | solution.py:14
  128.1 38.4 %collective-permute-done.4 = f32[8,17408]{1,0:T(8,128)S(1)} collective-permute-done((f32[8,17408]{1,0:T(8,128)S(1)}, f32[8,17408]{1,0:T(8,128)S(1)}, u32[]{:S(2)}, u32[]{:S(2)}) %collective-permute-start.4) | collective-permute-done | bytes 557088 | tf_op jit(solution)/shard_map/ppermute | solution.py:14
  168.1 18.2 %collective-permute-done.5 = f32[8,17408]{1,0:T(8,128)} collective-permute-done((f32[8,17408]{1,0:T(8,128)S(1)}, f32[8,17408]{1,0:T(8,128)}, u32[]{:S(2)}, u32[]{:S(2)}) %collective-permute-start.5) | collective-permute-done | bytes 557088 | tf_op jit(solution)/shard_map/ppermute | solution.py:14
  188.4 12.0 %all_gather.11 = bf16[8,2,2048]{2,0,1:T(8,128)(2,1)S(1)} all-gather(bf16[8,2,512]{2,0,1:T(8,128)(2,1)S(1)} %bitcast.193), channel_id=1, replica_groups=mesh['grp'=64,'head'=4] {'head'}, dimensions={2}, use_global_device_ids=true | all-gather | bytes 81920 | tf_op jit(solution)/shard_map/all_gather | solution.py:232
  203.6 1.5 reshape.292
  205.2 1.9 fusion.105
  207.1 1.9 fusion.103
  209.1 1.8 fusion.101
  211.0 4.1 %fusion.36 = (f32[8,4,64,64]{3,2,1,0:T(8,128)}, f32[8,4,64,64]{3,2,1,0:T(8,128)S(1)}) fusion(f32[8,4,64]{2,1,0:T(4,128)S(1)} %copy-done.13, f32[8,4,64]{2,1,0:T(4,128)S(1)} %copy.94, f32[8,4,64]{2,1,0:T(4,128)S(1)} %copy.93, f32[8,4,64]{2,1,0:T(4,128)S(1)} %copy-done.12, f32[8,4,64]{2,1,0:T(4,128)S(1)} %copy.92, f32[8,4,64]{2,1,0:T(4,128)S(1)} %copy.91, ...), kind=kLoop, calls=%fused_computation.49 | loop fusion | flops 2359296 | bytes 2195504 | tf_op jit(solution)/shard_map/jit(_where)/select_n | solution.py:150
  215.2 2.8 fusion.34
  218.0 2.3 fusion.30
  220.3 1.7 fusion.26
  225.3 40.4 %all-reduce.3.cloned.1.call-done = bf16[8,4,2048]{2,1,0:T(4,128)(2,1)} async-done(((bf16[8,4,2048]{2,1,0:T(4,128)(2,1)}), bf16[8,4,2048]{2,1,0:T(4,128)(2,1)}) %all-reduce.3.cloned.1.call-update) | async-done | bytes 131088 | tf_op jit(solution)/shard_map/psum | solution.py:270
  267.8 2.7 fusion.10
  270.6 3.4 %fusion.3 = bf16[2048,32]{0,1:T(8,128)(2,1)} fusion(bf16[32,896]{1,0:T(8,128)(2,1)S(1)} %reshape.296, bf16[896,2048]{1,0:T(8,128)(2,1)} %param.43), kind=kOutput, calls=%fused_computation.12 | convolution fusion | flops 117506048 | bytes 3858432 | tf_op jit(solution)/shard_map/dot_general | solution.py:290
  274.7 22.9 %reduce-scatter.2.cloned.1.call-done = bf16[512,32]{0,1:T(8,128)(2,1)} async-done(((bf16[2048,32]{0,1:T(8,128)(2,1)}), bf16[512,32]{0,1:T(8,128)(2,1)}) %reduce-scatter.2.cloned.1.call-update) | async-done | bytes 32784 | tf_op jit(solution)/shard_map/reduce_scatter | solution.py:289
  (266 shorter events, 58.4 us)
Async XLA Ops:
  7.2 216.6 %copy-start = (bf16[256,2048]{1,0:T(8,128)(2,1)S(1)}, bf16[256,2048]{1,0:T(8,128)(2,1)}, u32[]{:S(2)}) copy-start(bf16[256,2048]{1,0:T(8,128)(2,1)} %param.41) | copy-start | bytes 3145732
  7.2 258.5 %all-reduce.3.cloned.1.call-start = ((), (), s32[]{:S(2)}) async-start(), calls=%async_computation.1 | async-start | bytes 262144 | tf_op jit(solution)/shard_map/psum | solution.py:270
  11.0 16.9 %copy-start.9 = (f32[2048]{0:T(1024)S(1)}, f32[2048]{0:T(1024)}, u32[]{:S(2)}) copy-start(f32[2048]{0:T(1024)} %param.30) | copy-start | bytes 24580
  11.8 26.7 %copy-start.17 = (bf16[64,256]{1,0:T(8,128)(2,1)S(1)}, bf16[64,256]{1,0:T(8,128)(2,1)}, u32[]{:S(2)}) copy-start(bf16[64,256]{1,0:T(8,128)(2,1)} %param.37) | copy-start | bytes 98308
  11.8 26.7 %copy-start.30 = (f32[256]{0:T(256)S(1)}, f32[256]{0:T(256)}, u32[]{:S(2)}) copy-start(f32[256]{0:T(256)} %param.38) | copy-start | bytes 3076
  12.7 15.4 %collective-permute-start = (f32[8,17408]{1,0:T(8,128)}, f32[8,17408]{1,0:T(8,128)S(1)}, u32[]{:S(2)}, u32[]{:S(2)}) collective-permute-start(f32[8,17408]{1,0:T(8,128)} %broadcast_select_fusion), channel_id=1, source_target_pairs={{0,252},{4,0},{8,4},{12,8},{16,12},{20,16},{24,20},{28,24},{32,28}... | collective-permute-start | bytes 1671176 | tf_op jit(solution)/shard_map/ppermute | solution.py:14
  13.5 187.6 %copy-start.19 = (pred[8]{0:T(512)(128)(4,1)}, pred[8]{0:T(512)(128)(4,1)S(1)}, u32[]{:S(2)}) copy-start(pred[8]{0:T(512)(128)(4,1)S(1)} %get-tuple-element.124) | copy-start | bytes 28
  14.7 25.4 %copy-start.21 = (f32[1,2048]{1,0:T(1,128)}, f32[1,2048]{1,0:T(1,128)S(1)}, u32[]{:S(2)}) copy-start(f32[1,2048]{1,0:T(1,128)S(1)} %get-tuple-element.101) | copy-start | bytes 24580
  28.1 12.0 %copy-start.5 = (f32[2,32,2048]{2,1,0:T(8,128)}, f32[2,32,2048]{2,1,0:T(8,128)S(1)}, u32[]{:S(2)}) copy-start(f32[2,32,2048]{2,1,0:T(8,128)S(1)} %fusion.133) | copy-start | bytes 1572868
  30.2 16.1 %copy-start.2 = (f32[8,17408]{1,0:T(8,128)}, f32[8,17408]{1,0:T(8,128)S(1)}, u32[]{:S(2)}) copy-start(f32[8,17408]{1,0:T(8,128)S(1)} %broadcast_select_fusion.1) | copy-start | bytes 1671172
  30.2 18.5 %collective-permute-start.1 = (f32[8,17408]{1,0:T(8,128)S(1)}, f32[8,17408]{1,0:T(8,128)}, u32[]{:S(2)}, u32[]{:S(2)}) collective-permute-start(f32[8,17408]{1,0:T(8,128)S(1)} %broadcast_select_fusion.1), channel_id=1, source_target_pairs={{0,248},{4,252},{8,0},{12,4},{16,8},{20,12},{24,16},{28,20},{32,24... | collective-permute-start | bytes 1671176 | tf_op jit(solution)/shard_map/ppermute | solution.py:14
  43.9 11.5 %copy-start.1 = (bf16[2048,256]{0,1:T(8,128)(2,1)}, bf16[2048,256]{0,1:T(8,128)(2,1)S(1)}, u32[]{:S(2)}) copy-start(bf16[2048,256]{0,1:T(8,128)(2,1)S(1)} %copy.81) | copy-start | bytes 3145732
  48.7 46.0 %copy-start.16 = (bf16[8,4,512]{2,1,0:T(4,128)(2,1)S(1)}, bf16[8,4,512]{2,1,0:T(4,128)(2,1)}, u32[]{:S(2)}) copy-start(bf16[8,4,512]{2,1,0:T(4,128)(2,1)} %param.23) | copy-start | bytes 98308
  50.0 58.1 %copy-start.35 = (s32[8]{0:T(128)S(1)}, s32[8]{0:T(128)}, u32[]{:S(2)}) copy-start(s32[8]{0:T(128)} %param.24) | copy-start | bytes 100
  50.0 56.6 %collective-permute-start.2 = (f32[8,17408]{1,0:T(8,128)S(1)}, f32[8,17408]{1,0:T(8,128)}, u32[]{:S(2)}, u32[]{:S(2)}) collective-permute-start(f32[8,17408]{1,0:T(8,128)S(1)} %broadcast_select_fusion.2), channel_id=1, source_target_pairs={{0,240},{4,244},{8,248},{12,252},{16,0},{20,4},{24,8},{28,12},{32,... | collective-permute-start | bytes 1671176 | tf_op jit(solution)/shard_map/ppermute | solution.py:14
  90.1 76.4 %copy-start.24 = (pred[8]{0:T(512)(128)(4,1)S(1)}, pred[8]{0:T(512)(128)(4,1)}, u32[]{:S(2)}) copy-start(pred[8]{0:T(512)(128)(4,1)} %get-tuple-element.125) | copy-start | bytes 28
  92.4 74.3 %copy-start.29 = (s32[8]{0:T(128)S(1)}, s32[8]{0:T(128)}, u32[]{:S(2)}) copy-start(s32[8]{0:T(128)} %get-tuple-element.87) | copy-start | bytes 100
  107.9 78.5 %copy-start.28 = (pred[8]{0:T(512)(128)(4,1)S(1)}, pred[8]{0:T(512)(128)(4,1)}, u32[]{:S(2)}) copy-start(pred[8]{0:T(512)(128)(4,1)} %get-tuple-element.89) | copy-start | bytes 28
  107.9 19.1 %collective-permute-start.3 = (f32[8,17408]{1,0:T(8,128)S(1)}, f32[8,17408]{1,0:T(8,128)S(1)}, u32[]{:S(2)}, u32[]{:S(2)}) collective-permute-start(f32[8,17408]{1,0:T(8,128)S(1)} %broadcast_select_fusion.3), channel_id=1, source_target_pairs={{0,224},{4,228},{8,232},{12,236},{16,240},{20,244},{24,248},{28,25... | collective-permute-start | bytes 1671176 | tf_op jit(solution)/shard_map/ppermute | solution.py:14
  127.1 39.4 %collective-permute-start.4 = (f32[8,17408]{1,0:T(8,128)S(1)}, f32[8,17408]{1,0:T(8,128)S(1)}, u32[]{:S(2)}, u32[]{:S(2)}) collective-permute-start(f32[8,17408]{1,0:T(8,128)S(1)} %broadcast_select_fusion.4), channel_id=1, source_target_pairs={{0,192},{4,196},{8,200},{12,204},{16,208},{20,212},{24,216},{28,22... | collective-permute-start | bytes 1671176 | tf_op jit(solution)/shard_map/ppermute | solution.py:14
  166.5 34.6 %copy-start.23 = (pred[8]{0:T(512)(128)(4,1)S(1)}, pred[8]{0:T(512)(128)(4,1)}, u32[]{:S(2)}) copy-start(pred[8]{0:T(512)(128)(4,1)} %get-tuple-element.86) | copy-start | bytes 28
  166.5 34.7 %copy-start.22 = (f32[1,2048]{1,0:T(1,128)S(1)}, f32[1,2048]{1,0:T(1,128)}, u32[]{:S(2)}) copy-start(f32[1,2048]{1,0:T(1,128)} %copy-done.21) | copy-start | bytes 24580
  166.5 34.7 %copy-start.36 = (bf16[2048,64]{0,1:T(8,128)(2,1)S(1)}, bf16[2048,64]{0,1:T(8,128)(2,1)}, u32[]{:S(2)}) copy-start(bf16[2048,64]{0,1:T(8,128)(2,1)} %param.36) | copy-start | bytes 786436
  166.6 19.7 %collective-permute-start.5 = (f32[8,17408]{1,0:T(8,128)S(1)}, f32[8,17408]{1,0:T(8,128)}, u32[]{:S(2)}, u32[]{:S(2)}) collective-permute-start(f32[8,17408]{1,0:T(8,128)S(1)} %broadcast_select_fusion.5), channel_id=1, source_target_pairs={{0,128},{4,132},{8,136},{12,140},{16,144},{20,148},{24,152},{28,15... | collective-permute-start | bytes 1671176 | tf_op jit(solution)/shard_map/ppermute | solution.py:14
  167.3 34.4 %copy-start.31 = (f32[256]{0:T(256)S(1)}, f32[256]{0:T(256)}, u32[]{:S(2)}) copy-start(f32[256]{0:T(256)} %param.38) | copy-start | bytes 3076
  207.1 8.0 %copy-start.20 = (f32[4,64]{1,0:T(4,128)S(1)}, f32[4,64]{1,0:T(4,128)}, u32[]{:S(2)}) copy-start(f32[4,64]{1,0:T(4,128)} %mul.345) | copy-start | bytes 3076
  207.1 8.0 %copy-start.25 = (pred[8]{0:T(512)(128)(4,1)S(1)}, pred[8]{0:T(512)(128)(4,1)}, u32[]{:S(2)}) copy-start(pred[8]{0:T(512)(128)(4,1)} %get-tuple-element.133) | copy-start | bytes 28
  207.1 8.0 %copy-start.26 = (pred[8]{0:T(512)(128)(4,1)S(1)}, pred[8]{0:T(512)(128)(4,1)}, u32[]{:S(2)}) copy-start(pred[8]{0:T(512)(128)(4,1)} %get-tuple-element.135) | copy-start | bytes 28
  220.3 46.7 %copy-start.14 = (f32[2048]{0:T(1024)S(1)}, f32[2048]{0:T(1024)}, u32[]{:S(2)}) copy-start(f32[2048]{0:T(1024)} %param.31) | copy-start | bytes 24580
  220.3 46.9 %copy-start.15 = (f32[1,2048]{1,0:T(1,128)S(1)}, f32[1,2048]{1,0:T(1,128)}, u32[]{:S(2)}) copy-start(f32[1,2048]{1,0:T(1,128)} %get-tuple-element.99) | copy-start | bytes 24580
  224.8 72.8 %reduce-scatter.2.cloned.1.call-start = ((), (), s32[]{:S(2)}) async-start(), calls=%async_computation.2 | async-start | bytes 163840 | tf_op jit(solution)/shard_map/reduce_scatter | solution.py:289
  270.5 27.9 %copy-start.32 = (pred[8,4]{1,0:T(8,128)(4,1)S(1)}, pred[8,4]{1,0:T(8,128)(4,1)}, u32[]{:S(2)}) copy-start(pred[8,4]{1,0:T(8,128)(4,1)} %iota_compare_fusion.1) | copy-start | bytes 100
  (14 other events, 62.7 us)
Sparse Core Ops, SparseCore 0:
  225.0 40.6 all-reduce.2
  274.2 23.3 reduce-scatter.1
where the time goes:
time: 309 us; the launch traced here: 306 us
  waiting for transfers between devices  138 us (45%)
  local copies, waits for them, and re-layouts  44.9 us (15%)
  blocking collectives  36.6 us (12%)
  other arithmetic  29.1 us (9%)
  matrix products  27 us (9%)
  between operations  14.9 us (5%)
  starting transfers between devices  14.1 us (5%)
    ppermute x6, waiting for transfers between devices, shifted_2(): return lax.ppermute(value, axis, pairs)  74.9 us
    psum x1, waiting for transfers between devices, on_device(): lax.psum(jnp.dot(flat_heads, attention_exit_projection, preferred_element...  40.4 us
    dynamic_slice x32, local copies, waits for them, and re-layouts, rebuild(): lax.scan(advance, start_state, (jnp.moveaxis(key_rows, 1, 0), jnp.moveaxi...  24.8 us
    reduce_scatter x1, waiting for transfers between devices, on_device(): lax.psum_scatter(lax.dot_general(feedforward_content_proj, flat_hidden, (...  22.9 us
    dot_general x9, matrix products, project(): result = jnp.dot(flat_rows, weight, preferred_element_type=jnp.float32)  15.1 us
    ppermute x6, starting transfers between devices, shifted_2(): return lax.ppermute(value, axis, pairs)  13.8 us
    all_gather x1, blocking collectives, on_device(): lax.all_gather(chosen, 'head', axis=2, tiled=True)  12.6 us
    all_gather x1, blocking collectives, on_device(): lax.all_gather(shift_part.astype(jnp.bfloat16), 'head', axis=2, tiled=True)  12 us
  transfers between devices with their start and end apart: 8, of which 5 were waited for; matrix products, arithmetic and copies ran while one was open for 18% of the time, Pallas kernels for 0%

commit v1 on v0

--- a/solution.py
+++ b/solution.py
@@ -6,6 +6,11 @@
 ATTENTION_WIDTH = 64
 REB = 2
 EPSILON = 1e-05
+
+
+def summed_here(x, axis):
+    parts = lax.all_gather(x, axis)
+    return jnp.sum(parts, axis=0)
 
 
 def shifted_2(value, axis, steps):
@@ -267,7 +272,7 @@
         grouped_layer_scaling,
     )
     flat_heads = grouped_results.reshape(-1, grouped_results.shape[-1])
-    mix_total = lax.psum(
+    mix_total = summed_here(
         jnp.dot(flat_heads, attention_exit_projection, preferred_element_type=jnp.float32).astype(
             jnp.bfloat16
         ),

time: 309 us -> 274 us (0.89)
  waiting for transfers between devices: 138 us -> 91.7 us
  blocking collectives: 36.6 us -> 49.6 us
    psum x1 -> x0, waiting for transfers between devices: 40.4 us -> none  [on_device(): lax.psum(jnp.dot(flat_heads, attention_exit_projection, preferred_element...]
    all_gather x0 -> x1, blocking collectives: none -> 13 us  [summed_here(): parts = lax.all_gather(x, axis)]
    reduce_scatter x1, waiting for transfers between devices: 22.9 us -> 16.8 us  [on_device(): lax.psum_scatter(lax.dot_general(feedforward_content_proj, flat_hidden, (...]
  transfers between devices with their start and end apart: 8 -> 7, of which waited for: 5 -> 4; matrix products, arithmetic and copies ran while one was open for 18% -> 20% of each run, Pallas kernels for 0% -> 0%
where the time goes in v1:
time: 274 us; the launch traced here: 271 us
  waiting for transfers between devices  91.7 us (33%)
  blocking collectives  49.6 us (18%)
  local copies, waits for them, and re-layouts  44.2 us (16%)
  other arithmetic  28.3 us (10%)
  matrix products  27 us (10%)
  between operations  14.9 us (5%)
  starting transfers between devices  13.9 us (5%)
    ppermute x6, waiting for transfers between devices, shifted_2(): return lax.ppermute(value, axis, pairs)  74.8 us
    dynamic_slice x32, local copies, waits for them, and re-layouts, rebuild(): lax.scan(advance, start_state, (jnp.moveaxis(key_rows, 1, 0), jnp.moveaxi...  24.8 us
    reduce_scatter x1, waiting for transfers between devices, on_device(): lax.psum_scatter(lax.dot_general(feedforward_content_proj, flat_hidden, (...  16.8 us
    dot_general x9, matrix products, project(): result = jnp.dot(flat_rows, weight, preferred_element_type=jnp.float32)  15.1 us
    ppermute x6, starting transfers between devices, shifted_2(): return lax.ppermute(value, axis, pairs)  13.8 us
    all_gather x1, blocking collectives, summed_here(): parts = lax.all_gather(x, axis)  13 us
    all_gather x1, blocking collectives, on_device(): lax.all_gather(chosen, 'head', axis=2, tiled=True)  12.6 us
    all_gather x1, blocking collectives, on_device(): lax.all_gather(shift_part.astype(jnp.bfloat16), 'head', axis=2, tiled=True)  12 us
  transfers between devices with their start and end apart: 7, of which 4 were waited for; matrix products, arithmetic and copies ran while one was open for 20% of the time, Pallas kernels for 0%

profile of v1, /device:TPU:8, one launch (start us, length us, event | category | flops | bytes accessed | tf_op | source)
XLA Modules:
  0.0 270.7 jit_solution(4720859952503252107)
XLA Ops:
  7.2 1.4 and_compare_fusion.5
  9.4 1.6 reshape.287
  15.0 12.6 %all_gather.16 = bf16[2,32,2048]{2,1,0:T(8,128)(2,1)S(1)} all-gather(bf16[2,32,512]{2,1,0:T(8,128)(2,1)S(1)} %copy.145), channel_id=1, replica_groups=mesh['grp'=64,'head'=4] {'head'}, dimensions={2}, use_global_device_ids=true | all-gather | bytes 327680 | tf_op jit(solution)/shard_map/all_gather | solution.py:235
  29.0 1.2 broadcast_select_fusion.1
  30.2 8.3 %collective-permute-start.1 = (f32[8,17408]{1,0:T(8,128)S(1)}, f32[8,17408]{1,0:T(8,128)}, u32[]{:S(2)}, u32[]{:S(2)}) collective-permute-start(f32[8,17408]{1,0:T(8,128)S(1)} %broadcast_select_fusion.1), channel_id=1, source_target_pairs={{0,248},{4,252},{8,0},{12,4},{16,8},{20,12},{24,16},{28,20},{32,24... | collective-permute-start | bytes 1671176 | tf_op jit(solution)/shard_map/ppermute | solution.py:19
  38.5 1.4 fusion.15
  40.1 2.3 copy.80
  42.4 1.5 copy.81
  43.9 2.4 convolution_bitcast_fusion.1
  46.3 2.4 convolution_bitcast_fusion
  48.7 1.4 broadcast_select_fusion.2
  50.1 5.3 %collective-permute-start.2 = (f32[8,17408]{1,0:T(8,128)S(1)}, f32[8,17408]{1,0:T(8,128)}, u32[]{:S(2)}, u32[]{:S(2)}) collective-permute-start(f32[8,17408]{1,0:T(8,128)S(1)} %broadcast_select_fusion.2), channel_id=1, source_target_pairs={{0,240},{4,244},{8,248},{12,252},{16,0},{20,4},{24,8},{28,12},{32,... | collective-permute-start | bytes 1671176 | tf_op jit(solution)/shard_map/ppermute | solution.py:19
  55.4 34.7 %while.11 = (s32[]{:T(128)}, f32[2,4,64,64]{3,2,1,0:T(8,128)S(1)}, f32[32,2,4,64]{3,2,1,0:T(4,128)S(1)}, f32[32,2,4,64]{3,0,2,1:T(8,128)S(1)}, f32[32,2,4,64]{3,0,2,1:T(8,128)}, /*index=5*/s32[]{:T(128)}, s32[]{:T(128)}) while((s32[]{:T(128)}, f32[2,4,64,64]{3,2,1,0:T(8,128)S(1)}, f32[32,2,4,64]{3,2,1,0:T(4,128)S(1)}, ...), condition=%wide.region_6.7_spmd.clone, body=%wide.region_5.6_spmd.clone.sunk | while | flops 131075 | bytes 280679 | solution.py:102
  91.0 1.3 mul.345
  92.4 2.3 copy.77
  94.7 12.0 %all_gather.15 = bf16[8,4,2048]{2,1,0:T(4,128)(2,1)S(1)} all-gather(bf16[8,4,512]{2,1,0:T(4,128)(2,1)S(1)} %copy-done.15), channel_id=1, replica_groups=mesh['grp'=64,'head'=4] {'head'}, dimensions={2}, use_global_device_ids=true | all-gather | bytes 163840 | tf_op jit(solution)/shard_map/all_gather | solution.py:234
  108.7 18.2 %collective-permute-done.3 = f32[8,17408]{1,0:T(8,128)S(1)} collective-permute-done((f32[8,17408]{1,0:T(8,128)S(1)}, f32[8,17408]{1,0:T(8,128)S(1)}, u32[]{:S(2)}, u32[]{:S(2)}) %collective-permute-start.3) | collective-permute-done | bytes 557088 | tf_op jit(solution)/shard_map/ppermute | solution.py:19
  128.1 38.4 %collective-permute-done.4 = f32[8,17408]{1,0:T(8,128)S(1)} collective-permute-done((f32[8,17408]{1,0:T(8,128)S(1)}, f32[8,17408]{1,0:T(8,128)S(1)}, u32[]{:S(2)}, u32[]{:S(2)}) %collective-permute-start.4) | collective-permute-done | bytes 557088 | tf_op jit(solution)/shard_map/ppermute | solution.py:19
  168.1 18.2 %collective-permute-done.5 = f32[8,17408]{1,0:T(8,128)} collective-permute-done((f32[8,17408]{1,0:T(8,128)S(1)}, f32[8,17408]{1,0:T(8,128)}, u32[]{:S(2)}, u32[]{:S(2)}) %collective-permute-start.5) | collective-permute-done | bytes 557088 | tf_op jit(solution)/shard_map/ppermute | solution.py:19
  188.4 12.0 %all_gather.17 = bf16[8,2,2048]{2,0,1:T(8,128)(2,1)S(1)} all-gather(bf16[8,2,512]{2,0,1:T(8,128)(2,1)S(1)} %bitcast.195), channel_id=1, replica_groups=mesh['grp'=64,'head'=4] {'head'}, dimensions={2}, use_global_device_ids=true | all-gather | bytes 81920 | tf_op jit(solution)/shard_map/all_gather | solution.py:237
  203.7 1.5 reshape.290
  205.2 1.9 fusion.105
  207.2 1.9 fusion.103
  209.2 1.8 fusion.101
  211.1 4.1 %fusion.36 = (f32[8,4,64,64]{3,2,1,0:T(8,128)}, f32[8,4,64,64]{3,2,1,0:T(8,128)S(1)}) fusion(f32[8,4,64]{2,1,0:T(4,128)S(1)} %copy-done.12, f32[8,4,64]{2,1,0:T(4,128)S(1)} %copy.94, f32[8,4,64]{2,1,0:T(4,128)S(1)} %copy.93, f32[8,4,64]{2,1,0:T(4,128)S(1)} %copy-done.11, f32[8,4,64]{2,1,0:T(4,128)S(1)} %copy.92, f32[8,4,64]{2,1,0:T(4,128)S(1)} %copy.91, ...), kind=kLoop, calls=%fused_computation.49 | loop fusion | flops 2359296 | bytes 2195504 | tf_op jit(solution)/shard_map/jit(_where)/select_n | solution.py:155
  215.2 2.8 %fusion.34 = f32[8,4,1,64]{3,2,1,0:T(1,128)S(1)} fusion(f32[8,4,64]{2,1,0:T(4,128)S(1)} %copy.94, f32[8,4,64]{2,1,0:T(4,128)S(1)} %copy.93, f32[8,4,64]{2,1,0:T(4,128)S(1)} %copy-done.11, f32[8,4,64]{2,1,0:T(4,128)S(1)} %copy.92, f32[8,4,64]{2,1,0:T(4,128)S(1)} %copy.91, f32[4,64]{1,0:T(4,128)S(1)} %copy-done.19, pred[8]{0:T(512)(128)(4,1)S(1)} %copy-done.26, ...), kind=kOutput, calls=%fused_computation.48 | convolution fusion | flops 3538944 | bytes 631832 | tf_op jit(solution)/shard_map/ghl,ghlm->ghm/dot_general | solution.py:147
  218.1 2.3 fusion.30
  220.3 1.7 fusion.26
  224.2 13.0 %all-gather = bf16[128,2048]{1,0:T(8,128)(2,1)S(1)} all-gather(bf16[32,2048]{1,0:T(8,128)(2,1)S(1)} %convolution_convert_fusion.1), channel_id=2, replica_groups=mesh['grp'=64,'head'=4] {'head'}, dimensions={0}, use_global_device_ids=true | all-gather | bytes 655360 | tf_op jit(solution)/shard_map/all_gather | solution.py:12
  238.6 2.7 fusion.10
  241.4 3.4 %fusion.3 = bf16[2048,32]{0,1:T(8,128)(2,1)} fusion(bf16[32,896]{1,0:T(8,128)(2,1)S(1)} %reshape.292, bf16[896,2048]{1,0:T(8,128)(2,1)} %param.43), kind=kOutput, calls=%fused_computation.12 | convolution fusion | flops 117506048 | bytes 3858432 | tf_op jit(solution)/shard_map/dot_general | solution.py:295
  245.5 16.8 %reduce-scatter.2.cloned.1.call-done = bf16[512,32]{0,1:T(8,128)(2,1)} async-done(((bf16[2048,32]{0,1:T(8,128)(2,1)}), bf16[512,32]{0,1:T(8,128)(2,1)}) %reduce-scatter.2.cloned.1.call-update) | async-done | bytes 32784 | tf_op jit(solution)/shard_map/reduce_scatter | solution.py:294
  (265 shorter events, 56.7 us)
Async XLA Ops:
  7.2 216.7 %copy-start = (bf16[256,2048]{1,0:T(8,128)(2,1)S(1)}, bf16[256,2048]{1,0:T(8,128)(2,1)}, u32[]{:S(2)}) copy-start(bf16[256,2048]{1,0:T(8,128)(2,1)} %param.41) | copy-start | bytes 3145732
  7.2 255.2 %reduce-scatter.2.cloned.1.call-start = ((), (), s32[]{:S(2)}) async-start(), calls=%async_computation.1 | async-start | bytes 163840 | tf_op jit(solution)/shard_map/reduce_scatter | solution.py:294
  11.0 16.9 %copy-start.8 = (f32[2048]{0:T(1024)S(1)}, f32[2048]{0:T(1024)}, u32[]{:S(2)}) copy-start(f32[2048]{0:T(1024)} %param.30) | copy-start | bytes 24580
  11.8 26.7 %copy-start.16 = (bf16[64,256]{1,0:T(8,128)(2,1)S(1)}, bf16[64,256]{1,0:T(8,128)(2,1)}, u32[]{:S(2)}) copy-start(bf16[64,256]{1,0:T(8,128)(2,1)} %param.37) | copy-start | bytes 98308
  11.8 26.7 %copy-start.29 = (f32[256]{0:T(256)S(1)}, f32[256]{0:T(256)}, u32[]{:S(2)}) copy-start(f32[256]{0:T(256)} %param.38) | copy-start | bytes 3076
  12.7 15.4 %collective-permute-start = (f32[8,17408]{1,0:T(8,128)}, f32[8,17408]{1,0:T(8,128)S(1)}, u32[]{:S(2)}, u32[]{:S(2)}) collective-permute-start(f32[8,17408]{1,0:T(8,128)} %broadcast_select_fusion), channel_id=1, source_target_pairs={{0,252},{4,0},{8,4},{12,8},{16,12},{20,16},{24,20},{28,24},{32,28}... | collective-permute-start | bytes 1671176 | tf_op jit(solution)/shard_map/ppermute | solution.py:19
  13.5 187.6 %copy-start.18 = (pred[8]{0:T(512)(128)(4,1)}, pred[8]{0:T(512)(128)(4,1)S(1)}, u32[]{:S(2)}) copy-start(pred[8]{0:T(512)(128)(4,1)S(1)} %get-tuple-element.124) | copy-start | bytes 28
  14.7 25.4 %copy-start.20 = (f32[1,2048]{1,0:T(1,128)}, f32[1,2048]{1,0:T(1,128)S(1)}, u32[]{:S(2)}) copy-start(f32[1,2048]{1,0:T(1,128)S(1)} %get-tuple-element.101) | copy-start | bytes 24580
  28.1 12.0 %copy-start.3 = (f32[2,32,2048]{2,1,0:T(8,128)}, f32[2,32,2048]{2,1,0:T(8,128)S(1)}, u32[]{:S(2)}) copy-start(f32[2,32,2048]{2,1,0:T(8,128)S(1)} %fusion.133) | copy-start | bytes 1572868
  30.2 16.1 %copy-start.2 = (f32[8,17408]{1,0:T(8,128)}, f32[8,17408]{1,0:T(8,128)S(1)}, u32[]{:S(2)}) copy-start(f32[8,17408]{1,0:T(8,128)S(1)} %broadcast_select_fusion.1) | copy-start | bytes 1671172
  30.2 18.5 %collective-permute-start.1 = (f32[8,17408]{1,0:T(8,128)S(1)}, f32[8,17408]{1,0:T(8,128)}, u32[]{:S(2)}, u32[]{:S(2)}) collective-permute-start(f32[8,17408]{1,0:T(8,128)S(1)} %broadcast_select_fusion.1), channel_id=1, source_target_pairs={{0,248},{4,252},{8,0},{12,4},{16,8},{20,12},{24,16},{28,20},{32,24... | collective-permute-start | bytes 1671176 | tf_op jit(solution)/shard_map/ppermute | solution.py:19
  43.9 11.5 %copy-start.1 = (bf16[2048,256]{0,1:T(8,128)(2,1)}, bf16[2048,256]{0,1:T(8,128)(2,1)S(1)}, u32[]{:S(2)}) copy-start(bf16[2048,256]{0,1:T(8,128)(2,1)S(1)} %copy.81) | copy-start | bytes 3145732
  48.7 46.0 %copy-start.15 = (bf16[8,4,512]{2,1,0:T(4,128)(2,1)S(1)}, bf16[8,4,512]{2,1,0:T(4,128)(2,1)}, u32[]{:S(2)}) copy-start(bf16[8,4,512]{2,1,0:T(4,128)(2,1)} %param.23) | copy-start | bytes 98308
  48.7 58.0 %copy-start.35 = (s32[8]{0:T(128)S(1)}, s32[8]{0:T(128)}, u32[]{:S(2)}) copy-start(s32[8]{0:T(128)} %param.24) | copy-start | bytes 100
  50.1 58.0 %copy-start.36 = (s32[8]{0:T(128)S(1)}, s32[8]{0:T(128)}, u32[]{:S(2)}) copy-start(s32[8]{0:T(128)} %param.24) | copy-start | bytes 100
  50.1 56.6 %collective-permute-start.2 = (f32[8,17408]{1,0:T(8,128)S(1)}, f32[8,17408]{1,0:T(8,128)}, u32[]{:S(2)}, u32[]{:S(2)}) collective-permute-start(f32[8,17408]{1,0:T(8,128)S(1)} %broadcast_select_fusion.2), channel_id=1, source_target_pairs={{0,240},{4,244},{8,248},{12,252},{16,0},{20,4},{24,8},{28,12},{32,... | collective-permute-start | bytes 1671176 | tf_op jit(solution)/shard_map/ppermute | solution.py:19
  90.1 76.4 %copy-start.23 = (pred[8]{0:T(512)(128)(4,1)S(1)}, pred[8]{0:T(512)(128)(4,1)}, u32[]{:S(2)}) copy-start(pred[8]{0:T(512)(128)(4,1)} %get-tuple-element.125) | copy-start | bytes 28
  92.4 74.3 %copy-start.28 = (s32[8]{0:T(128)S(1)}, s32[8]{0:T(128)}, u32[]{:S(2)}) copy-start(s32[8]{0:T(128)} %get-tuple-element.87) | copy-start | bytes 100
  107.8 78.5 %copy-start.27 = (pred[8]{0:T(512)(128)(4,1)S(1)}, pred[8]{0:T(512)(128)(4,1)}, u32[]{:S(2)}) copy-start(pred[8]{0:T(512)(128)(4,1)} %get-tuple-element.89) | copy-start | bytes 28
  107.8 19.1 %collective-permute-start.3 = (f32[8,17408]{1,0:T(8,128)S(1)}, f32[8,17408]{1,0:T(8,128)S(1)}, u32[]{:S(2)}, u32[]{:S(2)}) collective-permute-start(f32[8,17408]{1,0:T(8,128)S(1)} %broadcast_select_fusion.3), channel_id=1, source_target_pairs={{0,224},{4,228},{8,232},{12,236},{16,240},{20,244},{24,248},{28,25... | collective-permute-start | bytes 1671176 | tf_op jit(solution)/shard_map/ppermute | solution.py:19
  127.1 39.4 %collective-permute-start.4 = (f32[8,17408]{1,0:T(8,128)S(1)}, f32[8,17408]{1,0:T(8,128)S(1)}, u32[]{:S(2)}, u32[]{:S(2)}) collective-permute-start(f32[8,17408]{1,0:T(8,128)S(1)} %broadcast_select_fusion.4), channel_id=1, source_target_pairs={{0,192},{4,196},{8,200},{12,204},{16,208},{20,212},{24,216},{28,22... | collective-permute-start | bytes 1671176 | tf_op jit(solution)/shard_map/ppermute | solution.py:19
  166.4 34.7 %copy-start.22 = (pred[8]{0:T(512)(128)(4,1)S(1)}, pred[8]{0:T(512)(128)(4,1)}, u32[]{:S(2)}) copy-start(pred[8]{0:T(512)(128)(4,1)} %get-tuple-element.86) | copy-start | bytes 28
  166.6 34.7 %copy-start.21 = (f32[1,2048]{1,0:T(1,128)S(1)}, f32[1,2048]{1,0:T(1,128)}, u32[]{:S(2)}) copy-start(f32[1,2048]{1,0:T(1,128)} %copy-done.20) | copy-start | bytes 24580
  166.6 34.7 %copy-start.37 = (bf16[2048,64]{0,1:T(8,128)(2,1)S(1)}, bf16[2048,64]{0,1:T(8,128)(2,1)}, u32[]{:S(2)}) copy-start(bf16[2048,64]{0,1:T(8,128)(2,1)} %param.36) | copy-start | bytes 786436
  166.6 19.7 %collective-permute-start.5 = (f32[8,17408]{1,0:T(8,128)S(1)}, f32[8,17408]{1,0:T(8,128)}, u32[]{:S(2)}, u32[]{:S(2)}) collective-permute-start(f32[8,17408]{1,0:T(8,128)S(1)} %broadcast_select_fusion.5), channel_id=1, source_target_pairs={{0,128},{4,132},{8,136},{12,140},{16,144},{20,148},{24,152},{28,15... | collective-permute-start | bytes 1671176 | tf_op jit(solution)/shard_map/ppermute | solution.py:19
  167.3 34.4 %copy-start.30 = (f32[256]{0:T(256)S(1)}, f32[256]{0:T(256)}, u32[]{:S(2)}) copy-start(f32[256]{0:T(256)} %param.38) | copy-start | bytes 3076
  207.2 8.0 %copy-start.19 = (f32[4,64]{1,0:T(4,128)S(1)}, f32[4,64]{1,0:T(4,128)}, u32[]{:S(2)}) copy-start(f32[4,64]{1,0:T(4,128)} %mul.345) | copy-start | bytes 3076
  220.3 17.4 %copy-start.13 = (f32[2048]{0:T(1024)S(1)}, f32[2048]{0:T(1024)}, u32[]{:S(2)}) copy-start(f32[2048]{0:T(1024)} %param.31) | copy-start | bytes 24580
  220.3 17.6 %copy-start.7 = (f32[8,1,2048]{2,1,0:T(1,128)S(1)}, f32[8,1,2048]{2,1,0:T(1,128)}, u32[]{:S(2)}) copy-start(f32[8,1,2048]{2,1,0:T(1,128)} %copy.95) | copy-start | bytes 196612
  220.3 17.6 %copy-start.14 = (f32[1,2048]{1,0:T(1,128)S(1)}, f32[1,2048]{1,0:T(1,128)}, u32[]{:S(2)}) copy-start(f32[1,2048]{1,0:T(1,128)} %get-tuple-element.99) | copy-start | bytes 24580
  220.3 17.6 %copy-start.33 = (pred[8,4]{1,0:T(8,128)(4,1)S(1)}, pred[8,4]{1,0:T(8,128)(4,1)}, u32[]{:S(2)}) copy-start(pred[8,4]{1,0:T(8,128)(4,1)} %iota_compare_fusion) | copy-start | bytes 100
  241.3 21.8 %copy-start.31 = (pred[8,4]{1,0:T(8,128)(4,1)S(1)}, pred[8,4]{1,0:T(8,128)(4,1)}, u32[]{:S(2)}) copy-start(pred[8,4]{1,0:T(8,128)(4,1)} %iota_compare_fusion.1) | copy-start | bytes 100
  (13 other events, 68.3 us)
Sparse Core Ops, SparseCore 0:
  245.0 17.3 reduce-scatter.1
